TPU v7x, 32 devices: a whole 2x2x4 slice. The times are simulated.
32 devices in a mesh: dp: 2 (over core), seq: 4 (over z), head: 4 (over y, x).
Axes of the slice: x: 2, y: 2, z: 4, core: 2. Of those that a mesh axis runs over, the one named last changes fastest.
Arguments:
- x_in: float32 [2, 512, 1024], P('dp', 'seq'), may hold values from -6 to 6
- cotangent: float32 [2, 512, 1024], P('dp', 'seq'), may hold values from -6 to 6
- attn_gain: bfloat16 [1024], P('seq'), may hold values from 0.25 to 1.75
- w_query: bfloat16 [1024, 512], P('seq', 'head'), may hold values from -0.1875 to 0.1875
- w_key: bfloat16 [1024, 512], P('seq', 'head'), may hold values from -0.1875 to 0.1875
- w_value: bfloat16 [1024, 1024], P('seq', 'head'), may hold values from -0.1875 to 0.1875
- w_outgate: bfloat16 [1024, 1024], P('seq', 'head'), may hold values from -0.1875 to 0.1875
- w_lowrank: bfloat16 [1024, 16], P('seq'), may hold values from -0.1875 to 0.1875
- w_forget: float32 [16, 512], replicated, may hold values from -1.5 to 1.5
- forget_bias: float32 [512], replicated, may hold values from -1 to 6
- group_gain: float32 [256], replicated, may hold values from 0.25 to 1.75
- w_output: bfloat16 [1024, 1024], P('head', 'seq'), may hold values from -0.375 to 0.375
- mlp_gain: bfloat16 [1024], P('seq'), may hold values from 0.25 to 1.75
- w_gate: bfloat16 [1024, 2816], P('seq', 'head'), may hold values from -0.1875 to 0.1875
- w_up: bfloat16 [1024, 2816], P('seq', 'head'), may hold values from -0.1875 to 0.1875
- w_down: bfloat16 [2816, 1024], P('head', 'seq'), may hold values from -0.109375 to 0.109375
Outputs:
- block_out: float32 [2, 512, 1024], P('dp', 'seq')
- grad_input: float32 [2, 512, 1024], P('dp', 'seq')
- grad_attn_gain: float32 [1024], P('seq')
- grad_query: float32 [1024, 512], P('seq', 'head')
- grad_key: float32 [1024, 512], P('seq', 'head')
- grad_value: float32 [1024, 1024], P('seq', 'head')
- grad_outgate: float32 [1024, 1024], P('seq', 'head')
- grad_lowrank: float32 [1024, 16], P('seq')
- grad_forget: float32 [16, 512], replicated
- grad_bias: float32 [512], replicated
- grad_group_gain: float32 [256], replicated
- grad_output: float32 [1024, 1024], P('head', 'seq')
- grad_mlp_gain: float32 [1024], P('seq')
- grad_gate: float32 [1024, 2816], P('seq', 'head')
- grad_up: float32 [1024, 2816], P('seq', 'head')
- grad_down: float32 [2816, 1024], P('head', 'seq')
All inputs are finite; a program needn't handle non-finite values.
Results may differ from a plain program's by a relative error of at most 0.0097.
Values may be sent and summed in bfloat16 or wider, within the bound.
A program may use at most 128 MiB of HBM per device.

v0:
```python
import jax
import jax.numpy as jnp
from jax import lax
from jax.sharding import PartitionSpec as P

DK = 128
DV = 256
SPAN = 64
epsilon = 1e-06
normalizer = 16.0
highest = lax.Precision.HIGHEST


def entering(part, axis, combine, identity, reverse):
    count = lax.axis_size(axis)
    place = lax.axis_index(axis)
    ahead = count - 1 - place if reverse else place
    gathered = jax.tree.map(lambda a: lax.all_gather(a, axis), part)
    state = jax.tree.map(lambda a, e: jnp.zeros_like(a) + jnp.asarray(e, a.dtype), part, identity)

    def one(step, state):
        source = count - 1 - step if reverse else step
        return combine(
            state, jax.tree.map(lambda a: lax.dynamic_index_in_dim(a, source, 0, False), gathered)
        )

    return lax.fori_loop(0, ahead, one, state)


def product(left, right):
    return jnp.dot(left, right, preferred_element_type=jnp.float32)


def rms_rows(inputs):
    return lax.rsqrt(jnp.mean(inputs * inputs, axis=-1, keepdims=True) + epsilon)


def norm_back(inputs, scale, gain, grad):
    scaled = gain * grad
    gain_terms = grad * inputs * scale
    input_grad = scale * scaled - inputs * scale**3 * jnp.mean(
        scaled * inputs, axis=-1, keepdims=True
    )
    return (gain_terms, input_grad)


def compose(earlier, later):
    return (earlier[0] * later[0], later[0][..., None] * earlier[1] + later[1])


def mixer_block(queries, keys_in, values_in, log_decay, start_state):
    block_len = min(SPAN, queries.shape[0])
    blocks = queries.shape[0] // block_len

    def cut(array):
        return array.reshape(blocks, block_len, array.shape[-1])

    lower = jnp.tril(jnp.ones((block_len, block_len), jnp.float32))

    def block_step(carried, pieces):
        query_blk, key_blk, value_blk, decay_blk = pieces
        running = jnp.cumsum(decay_blk, axis=0)
        from_state = jnp.dot(query_blk * jnp.exp(running), carried, precision=highest)
        spread = (
            jnp.exp(jnp.minimum(running[:, None, :] - running[None, :, :], 0.0)) * lower[:, :, None]
        )
        scores = jnp.einsum("id,jd,ijd->ij", query_blk, key_blk, spread, precision=highest)
        inside = jnp.dot(scores, value_blk, precision=highest)
        ending = running[-1]
        weighted = key_blk * jnp.exp(ending[None, :] - running)
        carried = jnp.exp(ending)[:, None] * carried + jnp.dot(
            weighted.T, value_blk, precision=highest
        )
        return (carried, from_state + inside)

    final_state, outputs = lax.scan(
        jax.checkpoint(block_step),
        start_state,
        (cut(queries), cut(keys_in), cut(values_in), cut(log_decay)),
    )
    return (outputs.reshape(queries.shape[0], values_in.shape[-1]), final_state)


def on_device(
    x_in,
    cotangent,
    attn_gain,
    w_query,
    w_key,
    w_value,
    w_outgate,
    w_lowrank,
    w_forget,
    forget_bias,
    group_gain,
    w_output,
    mlp_gain,
    w_gate,
    w_up,
    w_down,
):
    (
        gain_one,
        wq_full,
        wk_full,
        wv_full,
        wg_full,
        wl_full,
        wo_full,
        gain_two,
        wgate_full,
        wup_full,
        wdown_full,
    ) = (
        lax.all_gather(attn_gain, "seq", axis=0, tiled=True),
        lax.all_gather(w_query, "seq", axis=0, tiled=True),
        lax.all_gather(w_key, "seq", axis=0, tiled=True),
        lax.all_gather(w_value, "seq", axis=0, tiled=True),
        lax.all_gather(w_outgate, "seq", axis=0, tiled=True),
        lax.all_gather(w_lowrank, "seq", axis=0, tiled=True),
        lax.all_gather(w_output, "seq", axis=1, tiled=True),
        lax.all_gather(mlp_gain, "seq", axis=0, tiled=True),
        lax.all_gather(w_gate, "seq", axis=0, tiled=True),
        lax.all_gather(w_up, "seq", axis=0, tiled=True),
        lax.all_gather(w_down, "seq", axis=1, tiled=True),
    )
    seqs_here, tok_here, width = x_in.shape
    total_rows = seqs_here * tok_here
    heads_here = wq_full.shape[1] // DK
    key_cols = heads_here * DK
    head_scale = DK ** (-0.5)
    head_pos = lax.axis_index("head")
    forget_cols = lax.dynamic_slice_in_dim(w_forget, head_pos * key_cols, key_cols, 1)
    bias_cols = lax.dynamic_slice_in_dim(forget_bias, head_pos * key_cols, key_cols, 0)
    gain_first = gain_one.astype(jnp.float32)
    gain_second = gain_two.astype(jnp.float32)

    def heads_of(array, size):
        return array.reshape(seqs_here, tok_here, heads_here, size).transpose(0, 2, 1, 3)

    def rows_of(array):
        return array.transpose(0, 2, 1, 3).reshape(total_rows, -1)

    flat_in = x_in.reshape(total_rows, width)
    flat_cot = cotangent.reshape(total_rows, width)
    scale_one = rms_rows(flat_in)
    normed_in = (flat_in * scale_one * gain_first).astype(jnp.bfloat16)
    q_rows = product(normed_in, wq_full)
    k_rows = product(normed_in, wk_full)
    v_rows = product(normed_in, wv_full)
    og_rows = product(normed_in, wg_full)
    low_rank = product(normed_in, wl_full)
    pre_gate = jnp.dot(low_rank, forget_cols, precision=highest) + bias_cols
    log_decay = jax.nn.log_sigmoid(pre_gate) / normalizer
    q_heads = heads_of(q_rows, DK)
    k_heads = heads_of(k_rows, DK)
    v_heads = heads_of(v_rows, DV)
    decay_heads = heads_of(log_decay, DK)
    running = jnp.cumsum(decay_heads, axis=2)
    ending = running[:, :, -1, :]
    decay_total = jnp.exp(ending)
    local_state = jnp.einsum(
        "shld,shlv->shdv",
        k_heads * jnp.exp(ending[:, :, None, :] - running),
        v_heads,
        precision=highest,
    )
    identity = (jnp.ones_like(decay_total), jnp.zeros_like(local_state))
    start_total, start_state = entering((decay_total, local_state), "seq", compose, identity, False)

    def mixed(q_part, k_part, v_part, d_part):
        return jax.vmap(jax.vmap(mixer_block))(
            q_part * head_scale, k_part, v_part, d_part, start_state
        )

    (o_heads, end_state), pullback = jax.vjp(mixed, q_heads, k_heads, v_heads, decay_heads)
    gate_heads = heads_of(og_rows, DV)
    scale_three = rms_rows(o_heads)
    gated_norm = o_heads * scale_three * group_gain
    gate_sig = jax.nn.sigmoid(gate_heads)
    gate_act = gate_heads * gate_sig
    mixed_out = rows_of(gated_norm * gate_act).astype(jnp.bfloat16)
    resid = flat_in + lax.psum(product(mixed_out, wo_full), "head")
    scale_two = rms_rows(resid)
    normed_mid = (resid * scale_two * gain_second).astype(jnp.bfloat16)
    gate_pre = product(normed_mid, wgate_full)
    up_pre = product(normed_mid, wup_full)
    gate_sigma = jax.nn.sigmoid(gate_pre)
    gate_silu = gate_pre * gate_sigma
    mlp_hidden = (gate_silu * up_pre).astype(jnp.bfloat16)
    result = resid + lax.psum(product(mlp_hidden, wdown_full).astype(jnp.bfloat16), "head").astype(
        jnp.float32
    )
    grad_out_b = flat_cot.astype(jnp.bfloat16)
    d_down = product(mlp_hidden.T, grad_out_b)
    d_hidden = product(grad_out_b, wdown_full.T)
    d_gate_pre = (d_hidden * up_pre * gate_sigma * (1.0 + gate_pre * (1.0 - gate_sigma))).astype(
        jnp.bfloat16
    )
    d_up_pre = (d_hidden * gate_silu).astype(jnp.bfloat16)
    d_gate = product(normed_mid.T, d_gate_pre)
    d_up = product(normed_mid.T, d_up_pre)
    d_normed_mid = lax.psum(
        product(d_gate_pre, wgate_full.T) + product(d_up_pre, wup_full.T), "head"
    )
    gain_terms, d_resid_norm = norm_back(resid, scale_two, gain_second, d_normed_mid)
    d_gain_two = jnp.sum(gain_terms, axis=0)
    d_resid = flat_cot + d_resid_norm
    d_resid_b = d_resid.astype(jnp.bfloat16)
    d_output = product(mixed_out.T, d_resid_b)
    d_mixed = heads_of(product(d_resid_b, wo_full.T), DV)
    d_norm_out = d_mixed * gate_act
    d_gate_heads = d_mixed * gated_norm * gate_sig * (1.0 + gate_heads * (1.0 - gate_sig))
    d_group = jnp.sum(d_norm_out * o_heads * scale_three, axis=(0, 1, 2))
    group_terms, d_o_heads = norm_back(o_heads, scale_three, group_gain, d_norm_out)
    state_grad = jnp.einsum(
        "shld,shlv->shdv", q_heads * head_scale * jnp.exp(running), d_o_heads, precision=highest
    )
    later_total, later_grad = entering((decay_total, state_grad), "seq", compose, identity, True)
    d_q, d_k, d_v, d_decay = pullback((d_o_heads, later_grad))
    d_pre = rows_of(d_decay) / normalizer * jax.nn.sigmoid(-pre_gate)
    d_bias = jnp.sum(d_pre, axis=0)
    d_forget = jnp.dot(low_rank.T, d_pre, precision=highest)
    d_low_part = jnp.dot(d_pre, forget_cols.T, precision=highest)
    d_q_b = rows_of(d_q).astype(jnp.bfloat16)
    d_k_b = rows_of(d_k).astype(jnp.bfloat16)
    d_v_b = rows_of(d_v).astype(jnp.bfloat16)
    d_og_b = rows_of(d_gate_heads).astype(jnp.bfloat16)
    d_query = product(normed_in.T, d_q_b)
    d_key = product(normed_in.T, d_k_b)
    d_value = product(normed_in.T, d_v_b)
    d_outgate = product(normed_in.T, d_og_b)
    d_in_part = (
        product(d_q_b, wq_full.T)
        + product(d_k_b, wk_full.T)
        + product(d_v_b, wv_full.T)
        + product(d_og_b, wg_full.T)
    )
    d_in_sum, d_low_sum = lax.psum((d_in_part, d_low_part), "head")
    d_low_b = d_low_sum.astype(jnp.bfloat16)
    d_lowrank = product(normed_in.T, d_low_b)
    d_normed_in = d_in_sum + product(d_low_b, wl_full.T)
    first_terms, d_in_norm = norm_back(flat_in, scale_one, gain_first, d_normed_in)
    d_gain_one = jnp.sum(first_terms, axis=0)
    grad_in = d_resid + d_in_norm
    parts = (
        lax.psum_scatter(d_gain_one, "seq", scatter_dimension=0, tiled=True),
        lax.psum_scatter(d_query, "seq", scatter_dimension=0, tiled=True),
        lax.psum_scatter(d_key, "seq", scatter_dimension=0, tiled=True),
        lax.psum_scatter(d_value, "seq", scatter_dimension=0, tiled=True),
        lax.psum_scatter(d_outgate, "seq", scatter_dimension=0, tiled=True),
        lax.psum_scatter(d_lowrank, "seq", scatter_dimension=0, tiled=True),
        lax.psum_scatter(d_output, "seq", scatter_dimension=1, tiled=True),
        lax.psum_scatter(d_gain_two, "seq", scatter_dimension=0, tiled=True),
        lax.psum_scatter(d_gate, "seq", scatter_dimension=0, tiled=True),
        lax.psum_scatter(d_up, "seq", scatter_dimension=0, tiled=True),
        lax.psum_scatter(d_down, "seq", scatter_dimension=1, tiled=True),
    )
    (
        s_gain_one,
        s_query,
        s_key,
        s_value,
        s_outgate,
        s_lowrank,
        s_output,
        s_gain_two,
        s_gate,
        s_up,
        s_down,
    ) = lax.psum(
        (
            parts[0],
            parts[1],
            parts[2],
            parts[3],
            parts[4],
            parts[5],
            parts[6],
            parts[7],
            parts[8],
            parts[9],
            parts[10],
        ),
        "dp",
    )
    forget_full = lax.dynamic_update_slice_in_dim(
        jnp.zeros(w_forget.shape, jnp.float32), d_forget, head_pos * key_cols, 1
    )
    bias_full = lax.dynamic_update_slice_in_dim(
        jnp.zeros(forget_bias.shape, jnp.float32), d_bias, head_pos * key_cols, 0
    )
    s_forget, s_bias, s_group = lax.psum((forget_full, bias_full, d_group), ("dp", "seq", "head"))
    return (
        result.reshape(seqs_here, tok_here, width),
        grad_in.reshape(seqs_here, tok_here, width),
        s_gain_one,
        s_query,
        s_key,
        s_value,
        s_outgate,
        s_lowrank,
        s_forget,
        s_bias,
        s_group,
        s_output,
        s_gain_two,
        s_gate,
        s_up,
        s_down,
    )


def solution(mesh):
    return jax.shard_map(
        on_device,
        mesh=mesh,
        in_specs=(
            P("dp", "seq", None),
            P("dp", "seq", None),
            P("seq"),
            P("seq", "head"),
            P("seq", "head"),
            P("seq", "head"),
            P("seq", "head"),
            P("seq", None),
            P(),
            P(),
            P(),
            P("head", "seq"),
            P("seq"),
            P("seq", "head"),
            P("seq", "head"),
            P("head", "seq"),
        ),
        out_specs=(
            P("dp", "seq", None),
            P("dp", "seq", None),
            P("seq"),
            P("seq", "head"),
            P("seq", "head"),
            P("seq", "head"),
            P("seq", "head"),
            P("seq", None),
            P(),
            P(),
            P(),
            P("head", "seq"),
            P("seq"),
            P("seq", "head"),
            P("seq", "head"),
            P("head", "seq"),
        ),
        check_vma=False,
    )
```

profile of v0, /device:TPU:0, one launch (start us, length us, event | category | flops | bytes accessed | tf_op | source)
XLA Modules:
  0.0 774.9 jit_solution(1150083508637122755)
XLA Ops:
  10.6 12.6 %all-gather.2 = bf16[4,1,256]{2,1,0:T(2,128)(2,1)S(1)} all-gather(bf16[1,1,256]{2,1,0:T(2,128)(2,1)S(1)} %reshape.777), channel_id=1, replica_groups=mesh['dp'=2,'seq'=4,'head'=4] {'seq'}, dimensions={0}, use_global_device_ids=true | all-gather | bytes 2560 | tf_op jit(solution)/shard_map/all_gather | solution.py:115
  23.2 13.3 %all_gather.52 = bf16[1024,16]{0,1:T(8,128)(2,1)S(1)} all-gather(bf16[256,16]{0,1:T(8,128)(2,1)} %param.31), channel_id=1, replica_groups=mesh['dp'=2,'seq'=4,'head'=4] {'seq'}, dimensions={0}, use_global_device_ids=true | all-gather | bytes 40960 | tf_op jit(solution)/shard_map/all_gather | solution.py:120
  39.2 15.9 %all_gather.55 = bf16[1024,256]{1,0:T(8,128)(2,1)S(1)} all-gather(bf16[256,256]{1,0:T(8,128)(2,1)S(1)} %copy-done.37), channel_id=1, replica_groups=mesh['dp'=2,'seq'=4,'head'=4] {'seq'}, dimensions={0}, use_global_device_ids=true | all-gather | bytes 655360 | tf_op jit(solution)/shard_map/all_gather | solution.py:118
  55.4 14.5 %all_gather.54 = bf16[1024,128]{1,0:T(8,128)(2,1)S(1)} all-gather(bf16[256,128]{1,0:T(8,128)(2,1)S(1)} %copy-done.41), channel_id=1, replica_groups=mesh['dp'=2,'seq'=4,'head'=4] {'seq'}, dimensions={0}, use_global_device_ids=true | all-gather | bytes 327680 | tf_op jit(solution)/shard_map/all_gather | solution.py:117
  70.5 15.0 %all-gather = f32[512,256]{1,0:T(8,128)S(1)} all-gather(f32[128,256]{1,0:T(8,128)S(1)} %fusion.104), channel_id=2, replica_groups=mesh['dp'=2,'seq'=4,'head'=4] {'seq'}, dimensions={0}, use_global_device_ids=true | all-gather | bytes 655360 | tf_op jit(solution)/shard_map/all_gather | solution.py:18
  85.5 8.7 %all_gather.53 = f32[4,1,1,128]{3,2,1,0:T(1,128)S(1)} all-gather(f32[1,1,1,128]{3,2,1,0:T(1,128)S(1)} %get-tuple-element.745), channel_id=1, replica_groups=mesh['dp'=2,'seq'=4,'head'=4] {'seq'}, dimensions={0}, use_global_device_ids=true | all-gather | bytes 2560 | tf_op jit(solution)/shard_map/all_gather | solution.py:18
  94.2 14.6 %all_gather.58 = bf16[1024,128]{1,0:T(8,128)(2,1)S(1)} all-gather(bf16[256,128]{1,0:T(8,128)(2,1)S(1)} %copy-done.42), channel_id=1, replica_groups=mesh['dp'=2,'seq'=4,'head'=4] {'seq'}, dimensions={0}, use_global_device_ids=true | all-gather | bytes 327680 | tf_op jit(solution)/shard_map/all_gather | solution.py:116
  109.6 6.8 while.70
  110.3 1.7 fusion.282
  113.7 1.7 fusion.282
  117.1 15.5 %all_gather.59 = bf16[1024,256]{1,0:T(8,128)(2,1)S(1)} all-gather(bf16[256,256]{1,0:T(8,128)(2,1)S(1)} %copy-done.38), channel_id=1, replica_groups=mesh['dp'=2,'seq'=4,'head'=4] {'seq'}, dimensions={0}, use_global_device_ids=true | all-gather | bytes 655360 | tf_op jit(solution)/shard_map/all_gather | solution.py:119
  132.6 14.8 %all_gather.60 = bf16[256,1024]{1,0:T(8,128)(2,1)S(1)} all-gather(bf16[256,256]{1,0:T(8,128)(2,1)S(1)} %copy-done.39), channel_id=1, replica_groups=mesh['dp'=2,'seq'=4,'head'=4] {'seq'}, dimensions={1}, use_global_device_ids=true | all-gather | bytes 655360 | tf_op jit(solution)/shard_map/all_gather | solution.py:121
  151.2 8.8 %all-gather.3 = bf16[4,1,256]{2,1,0:T(2,128)(2,1)S(1)} all-gather(bf16[1,1,256]{2,1,0:T(2,128)(2,1)S(1)} %reshape.779), channel_id=1, replica_groups=mesh['dp'=2,'seq'=4,'head'=4] {'seq'}, dimensions={0}, use_global_device_ids=true | all-gather | bytes 2560 | tf_op jit(solution)/shard_map/all_gather | solution.py:122
  161.1 32.6 %all-reduce.13.cloned.1.call-done = f32[128,1024]{1,0:T(8,128)} async-done(((f32[128,1024]{1,0:T(8,128)}), f32[128,1024]{1,0:T(8,128)}) %all-reduce.13.cloned.1.call-update) | async-done | bytes 524304 | tf_op jit(solution)/shard_map/psum | solution.py:183
  195.6 2.7 fusion.132
  198.3 22.5 %all-gather.10.cloned.1.call-done = bf16[1024,704]{0,1:T(8,128)(2,1)} async-done(((bf16[256,704]{0,1:T(8,128)(2,1)}), bf16[1024,704]{0,1:T(8,128)(2,1)}) %all-gather.10.cloned.1.call-update) | async-done | bytes 1441808 | tf_op jit(solution)/shard_map/all_gather | solution.py:124
  220.8 2.6 fusion.133
  223.4 32.5 %all-gather.12.cloned.1.call-done = bf16[704,1024]{1,0:T(8,128)(2,1)} async-done(((bf16[704,256]{1,0:T(8,128)(2,1)}), bf16[704,1024]{1,0:T(8,128)(2,1)}) %all-gather.12.cloned.1.call-update) | async-done | bytes 1441808 | tf_op jit(solution)/shard_map/all_gather | solution.py:125
  255.9 2.2 multiply_convert_fusion.2
  260.9 2.5 convolution_convert_fusion
  263.4 40.4 %all-reduce.17.cloned.1.call-done = f32[128,1024]{1,0:T(8,128)} async-done(((f32[128,1024]{1,0:T(8,128)}), f32[128,1024]{1,0:T(8,128)}) %all-reduce.17.cloned.1.call-update) | async-done | bytes 524304 | tf_op jit(solution)/shard_map/psum | solution.py:203
  303.8 1.8 multiply_reduce_fusion.1
  305.6 44.8 %all-reduce.15.cloned.1.call-done = bf16[128,1024]{1,0:T(8,128)(2,1)} async-done(((bf16[128,1024]{1,0:T(8,128)(2,1)}), bf16[128,1024]{1,0:T(8,128)(2,1)}) %all-reduce.15.cloned.1.call-update) | async-done | bytes 262160 | tf_op jit(solution)/shard_map/psum | solution.py:191
  350.4 2.3 bitcast_add_fusion.7
  352.7 2.6 fusion.94
  355.7 15.3 %all-gather.1 = f32[512,256]{1,0:T(8,128)S(1)} all-gather(f32[128,256]{1,0:T(8,128)S(1)} %fusion.107), channel_id=3, replica_groups=mesh['dp'=2,'seq'=4,'head'=4] {'seq'}, dimensions={0}, use_global_device_ids=true | all-gather | bytes 655360 | tf_op jit(solution)/shard_map/all_gather | solution.py:18
  371.0 2.6 while.69
  374.3 19.5 %while.71 = (s32[]{:T(128)}, f32[1,1,128,256]{2,3,1,0:T(8,128)S(1)}, f32[2,1,1,64,128]{4,3,2,1,0:T(8,128)S(1)}, bf16[2,1,1,64,128]{4,3,2,1,0:T(8,128)(2,1)}, bf1...) while((s32[]{:T(128)}, ...), condition=%wide.region_23.24_spmd.clone.clone, body=%wide.region_16.23_spmd.clone.sunk.clone | while | flops 141848576 | bytes 4776213 | solution.py:76
  379.7 2.3 fusion.303
  389.4 2.3 fusion.303
  395.8 1.8 fusion.137
  402.0 2.1 fusion.140
  405.0 2.1 fusion.141
  408.2 2.2 fusion.124
  413.6 9.2 %psum.137 = bf16[128,16]{0,1:T(8,128)(2,1)S(1)} all-reduce(f32[128,16]{0,1:T(8,128)S(1)} %fusion.111), channel_id=1, replica_groups=mesh['dp'=2,'seq'=4,'head'=4] {'head'}, use_global_device_ids=true, to_apply=%region_25.26 | all-reduce | flops 2048 | bytes 12288 | tf_op jit(solution)/shard_map/psum | solution.py:239
  423.7 15.4 %reduce-scatter.12.cloned.1.call-done = f32[256,128]{1,0:T(8,128)} async-done(((f32[1024,128]{1,0:T(8,128)}), f32[256,128]{1,0:T(8,128)}) %reduce-scatter.12.cloned.1.call-update) | async-done | bytes 131088 | tf_op jit(solution)/shard_map/reduce_scatter | solution.py:249
  439.2 27.9 %reduce-scatter.20.cloned.1.call-done = f32[256,256]{1,0:T(8,128)} async-done(((f32[256,1024]{1,0:T(8,128)}), f32[256,256]{1,0:T(8,128)}) %reduce-scatter.20.cloned.1.call-update) | async-done | bytes 262160 | tf_op jit(solution)/shard_map/reduce_scatter | solution.py:253
  467.1 27.9 %reduce-scatter.14.cloned.1.call-done = f32[256,256]{1,0:T(8,128)} async-done(((f32[1024,256]{1,0:T(8,128)}), f32[256,256]{1,0:T(8,128)}) %reduce-scatter.14.cloned.1.call-update) | async-done | bytes 262160 | tf_op jit(solution)/shard_map/reduce_scatter | solution.py:250
  495.0 27.9 %reduce-scatter.16.cloned.1.call-done = f32[256,256]{1,0:T(8,128)} async-done(((f32[1024,256]{1,0:T(8,128)}), f32[256,256]{1,0:T(8,128)}) %reduce-scatter.16.cloned.1.call-update) | async-done | bytes 262160 | tf_op jit(solution)/shard_map/reduce_scatter | solution.py:251
  522.9 57.0 %reduce-scatter.22.cloned.1.call-done = f32[256,704]{0,1:T(8,128)} async-done(((f32[1024,704]{0,1:T(8,128)}), f32[256,704]{0,1:T(8,128)}) %reduce-scatter.22.cloned.1.call-update) | async-done | bytes 720912 | tf_op jit(solution)/shard_map/reduce_scatter | solution.py:255
  579.9 58.4 %reduce-scatter.24.cloned.1.call-done = f32[256,704]{0,1:T(8,128)} async-done(((f32[1024,704]{0,1:T(8,128)}), f32[256,704]{0,1:T(8,128)}) %reduce-scatter.24.cloned.1.call-update) | async-done | bytes 720912 | tf_op jit(solution)/shard_map/reduce_scatter | solution.py:256
  638.2 58.2 %reduce-scatter.26.cloned.1.call-done = f32[704,256]{1,0:T(8,128)} async-done(((f32[704,1024]{1,0:T(8,128)}), f32[704,256]{1,0:T(8,128)}) %reduce-scatter.26.cloned.1.call-update) | async-done | bytes 720912 | tf_op jit(solution)/shard_map/reduce_scatter | solution.py:257
  698.2 40.7 %all-reduce.3 = (f32[16,512]{1,0:T(8,128)}, f32[512]{0:T(512)}, f32[256]{0:T(256)}) all-reduce(f32[16,512]{1,0:T(8,128)S(1)} %convolution_dynamic-update-slice_fusion, f32[512]{0:T(512)S(1)} %dynamic_update_slice.52, f32[256]{0:T(256)S(1)} %copy-done.48), channel_id=1, replica_groups=mesh['dp'=2,'seq'=4,'head'=4] {'dp','seq','head'}, use_global_device_ids=true, to_apply=%region_40.41 | all-reduce | flops 8960 | bytes 71680 | tf_op jit(solution)/shard_map/psum | solution.py:293
  740.3 10.8 %all-reduce.4 = (f32[1024]{0:T(1024)S(1)}, f32[1024]{0:T(1024)S(1)}) all-reduce(f32[1024]{0:T(1024)S(1)} %get-tuple-element.643, f32[1024]{0:T(1024)S(1)} %copy-done.43), channel_id=4, replica_groups=mesh['dp'=2,'seq'=4,'head'=4] {'seq'}, use_global_device_ids=true, to_apply=%region_28.29.clone | all-reduce | flops 2048 | bytes 16384
  751.3 4.6 all-reduce.5
  756.9 1.7 copy.186
  760.1 1.7 copy.188
  761.9 1.7 copy.189
  (301 shorter events, 59.5 us)
Async XLA Ops:
  8.0 30.6 %copy-start = (f32[16,512]{1,0:T(8,128)S(1)}, f32[16,512]{1,0:T(8,128)}, u32[]{:S(2)}) copy-start(f32[16,512]{1,0:T(8,128)} %param.32) | copy-start | bytes 98308
  8.0 31.2 %copy-start.37 = (bf16[256,256]{1,0:T(8,128)(2,1)S(1)}, bf16[256,256]{1,0:T(8,128)(2,1)}, u32[]{:S(2)}) copy-start(bf16[256,256]{1,0:T(8,128)(2,1)} %param.29) | copy-start | bytes 393220
  8.0 47.3 %copy-start.41 = (bf16[256,128]{1,0:T(8,128)(2,1)S(1)}, bf16[256,128]{1,0:T(8,128)(2,1)}, u32[]{:S(2)}) copy-start(bf16[256,128]{1,0:T(8,128)(2,1)} %param.28) | copy-start | bytes 196612
  8.0 185.7 %all-reduce.13.cloned.1.call-start = ((), (), s32[]{:S(2)}) async-start(), calls=%async_computation.9 | async-start | bytes 1048576 | tf_op jit(solution)/shard_map/psum | solution.py:183
  9.9 250.8 %copy-start.44 = (f32[128]{0:T(128)}, f32[128]{0:T(128)S(1)}, u32[]{:S(2)}) copy-start(f32[128]{0:T(128)S(1)} %get-tuple-element.747) | copy-start | bytes 1540
  39.0 55.2 %copy-start.24 = (f32[128,128]{1,0:T(8,128)}, f32[128,128]{1,0:T(8,128)S(1)}, u32[]{:S(2)}) copy-start(f32[128,128]{1,0:T(8,128)S(1)} %convolution_add_fusion.7) | copy-start | bytes 196612
  55.4 38.8 %copy-start.42 = (bf16[256,128]{1,0:T(8,128)(2,1)S(1)}, bf16[256,128]{1,0:T(8,128)(2,1)}, u32[]{:S(2)}) copy-start(bf16[256,128]{1,0:T(8,128)(2,1)} %param.27) | copy-start | bytes 196612
  69.9 24.3 %copy-start.7 = (bf16[1024,128]{1,0:T(8,128)(2,1)}, bf16[1024,128]{1,0:T(8,128)(2,1)S(1)}, u32[]{:S(2)}) copy-start(bf16[1024,128]{1,0:T(8,128)(2,1)S(1)} %all_gather.54) | copy-start | bytes 786436
  94.2 15.3 %copy-start.46 = (f32[4,1,1,128]{3,2,1,0:T(1,128)}, f32[4,1,1,128]{3,2,1,0:T(1,128)S(1)}, u32[]{:S(2)}) copy-start(f32[4,1,1,128]{3,2,1,0:T(1,128)S(1)} %get-tuple-element.1287) | copy-start | bytes 6148
  109.1 8.0 %copy-start.38 = (bf16[256,256]{1,0:T(8,128)(2,1)S(1)}, bf16[256,256]{1,0:T(8,128)(2,1)}, u32[]{:S(2)}) copy-start(bf16[256,256]{1,0:T(8,128)(2,1)} %param.30) | copy-start | bytes 393220
  109.1 23.5 %copy-start.39 = (bf16[256,256]{1,0:T(8,128)(2,1)S(1)}, bf16[256,256]{1,0:T(8,128)(2,1)}, u32[]{:S(2)}) copy-start(bf16[256,256]{1,0:T(8,128)(2,1)} %param.35) | copy-start | bytes 393220
  109.1 38.3 %copy-start.47 = (f32[256]{0:T(256)S(1)}, f32[256]{0:T(256)}, u32[]{:S(2)}) copy-start(f32[256]{0:T(256)} %param.34) | copy-start | bytes 3076
  116.4 33.0 %copy-start.29 = (f32[2,1,1,64,256]{4,3,2,1,0:T(8,128)}, f32[2,1,1,64,256]{4,3,2,1,0:T(8,128)S(1)}, u32[]{:S(2)}) copy-start(f32[2,1,1,64,256]{4,3,2,1,0:T(8,128)S(1)} %get-tuple-element.459) | copy-start | bytes 393220
  117.1 43.5 %copy-start.50 = (f32[128]{0:T(128)}, f32[128]{0:T(128)S(1)}, u32[]{:S(2)}) copy-start(f32[128]{0:T(128)S(1)} %rsqrt.38) | copy-start | bytes 1540
  132.6 17.9 %copy-start.9 = (bf16[1024,256]{1,0:T(8,128)(2,1)}, bf16[1024,256]{1,0:T(8,128)(2,1)S(1)}, u32[]{:S(2)}) copy-start(bf16[1024,256]{1,0:T(8,128)(2,1)S(1)} %all_gather.59) | copy-start | bytes 1572868
  147.4 47.5 %copy-start.11 = (bf16[256,1024]{1,0:T(8,128)(2,1)}, bf16[256,1024]{1,0:T(8,128)(2,1)S(1)}, u32[]{:S(2)}) copy-start(bf16[256,1024]{1,0:T(8,128)(2,1)S(1)} %all_gather.60) | copy-start | bytes 1572868
  147.4 46.3 %copy-start.1 = (f32[1,128,1024]{2,1,0:T(8,128)S(1)}, f32[1,128,1024]{2,1,0:T(8,128)}, u32[]{:S(2)}) copy-start(f32[1,128,1024]{2,1,0:T(8,128)} %param.24) | copy-start | bytes 1572868
  148.3 12.8 %copy-start.34 = (bf16[128,256]{1,0:T(8,128)(2,1)}, bf16[128,256]{1,0:T(8,128)(2,1)S(1)}, u32[]{:S(2)}) copy-start(bf16[128,256]{1,0:T(8,128)(2,1)S(1)} %get-tuple-element.750) | copy-start | bytes 196612
  149.4 46.2 %all-gather.8.cloned.1.call-start = ((), (), s32[]{:S(2)}) async-start(), calls=%async_computation.10 | async-start | bytes 1802240 | tf_op jit(solution)/shard_map/all_gather | solution.py:123
  149.9 70.9 %all-gather.10.cloned.1.call-start = ((), (), s32[]{:S(2)}) async-start(), calls=%async_computation.11 | async-start | bytes 1802240 | tf_op jit(solution)/shard_map/all_gather | solution.py:124
  150.5 105.4 %all-gather.12.cloned.1.call-start = ((), (), s32[]{:S(2)}) async-start(), calls=%async_computation.12 | async-start | bytes 1802240 | tf_op jit(solution)/shard_map/all_gather | solution.py:125
  151.1 152.7 %all-reduce.17.cloned.1.call-start = ((), (), s32[]{:S(2)}) async-start(), calls=%async_computation.14 | async-start | bytes 1048576 | tf_op jit(solution)/shard_map/psum | solution.py:203
  195.5 60.4 %copy-start.12 = (f32[1,128,1024]{2,1,0:T(8,128)S(1)}, f32[1,128,1024]{2,1,0:T(8,128)}, u32[]{:S(2)}) copy-start(f32[1,128,1024]{2,1,0:T(8,128)} %param.25) | copy-start | bytes 1572868
  260.1 90.3 %all-reduce.15.cloned.1.call-start = ((), (), s32[]{:S(2)}) async-start(), calls=%async_computation.13 | async-start | bytes 524288 | tf_op jit(solution)/shard_map/psum | solution.py:191
  263.3 89.4 %copy-start.30 = (f32[2,1,1,64,256]{4,3,2,1,0:T(8,128)S(1)}, f32[2,1,1,64,256]{4,3,2,1,0:T(8,128)}, u32[]{:S(2)}) copy-start(f32[2,1,1,64,256]{4,3,2,1,0:T(8,128)} %copy-done.29) | copy-start | bytes 393220
  263.3 89.4 %copy-start.51 = (f32[128]{0:T(128)S(1)}, f32[128]{0:T(128)}, u32[]{:S(2)}) copy-start(f32[128]{0:T(128)} %copy-done.50) | copy-start | bytes 1540
  263.4 160.4 %reduce-scatter.10.cloned.1.call-start = ((), (), s32[]{:S(2)}) async-start(), calls=%async_computation.16 | async-start | bytes 655360 | tf_op jit(solution)/shard_map/reduce_scatter | solution.py:248
  355.4 15.6 %copy-start.4 = (f32[128,256]{1,0:T(8,128)}, f32[128,256]{1,0:T(8,128)S(1)}, u32[]{:S(2)}) copy-start(f32[128,256]{1,0:T(8,128)S(1)} %fusion.91) | copy-start | bytes 393220
  376.6 6.6 copy-start.26
  386.3 6.6 copy-start.26
  395.8 43.4 %reduce-scatter.12.cloned.1.call-start = ((), (), s32[]{:S(2)}) async-start(), calls=%async_computation.17 | async-start | bytes 655360 | tf_op jit(solution)/shard_map/reduce_scatter | solution.py:249
  397.7 69.4 %reduce-scatter.20.cloned.1.call-start = ((), (), s32[]{:S(2)}) async-start(), calls=%async_computation.21 | async-start | bytes 1310720 | tf_op jit(solution)/shard_map/reduce_scatter | solution.py:253
  399.1 95.8 %reduce-scatter.14.cloned.1.call-start = ((), (), s32[]{:S(2)}) async-start(), calls=%async_computation.18 | async-start | bytes 1310720 | tf_op jit(solution)/shard_map/reduce_scatter | solution.py:250
  400.5 122.3 %reduce-scatter.16.cloned.1.call-start = ((), (), s32[]{:S(2)}) async-start(), calls=%async_computation.19 | async-start | bytes 1310720 | tf_op jit(solution)/shard_map/reduce_scatter | solution.py:251
  401.9 178.0 %reduce-scatter.22.cloned.1.call-start = ((), (), s32[]{:S(2)}) async-start(), calls=%async_computation.22 | async-start | bytes 3604480 | tf_op jit(solution)/shard_map/reduce_scatter | solution.py:255
  404.1 234.1 %reduce-scatter.24.cloned.1.call-start = ((), (), s32[]{:S(2)}) async-start(), calls=%async_computation.23 | async-start | bytes 3604480 | tf_op jit(solution)/shard_map/reduce_scatter | solution.py:256
  407.2 289.3 %reduce-scatter.26.cloned.1.call-start = ((), (), s32[]{:S(2)}) async-start(), calls=%async_computation.24 | async-start | bytes 3604480 | tf_op jit(solution)/shard_map/reduce_scatter | solution.py:257
  410.4 328.5 %all-reduce.19.cloned.1.call-start = ((), (), s32[]{:S(2)}) async-start(), calls=%async_computation.15 | async-start | bytes 1048576 | tf_op jit(solution)/shard_map/psum | solution.py:239
  413.3 283.2 %copy-start.54 = (u32[32]{0:T(128)S(1)}, u32[32]{0:T(128)}, u32[]{:S(2)}) copy-start(u32[32]{0:T(128)} %constant.207) | copy-start | bytes 388
  413.3 284.9 %copy-start.48 = (f32[256]{0:T(256)S(1)}, f32[256]{0:T(256)}, u32[]{:S(2)}) copy-start(f32[256]{0:T(256)} %get-tuple-element.645) | copy-start | bytes 3076
  413.3 325.6 %copy-start.45 = (f32[128]{0:T(128)S(1)}, f32[128]{0:T(128)}, u32[]{:S(2)}) copy-start(f32[128]{0:T(128)} %copy-done.44) | copy-start | bytes 1540
  413.3 338.0 %reduce-scatter.18.cloned.1.call-start = ((), (), s32[]{:S(2)}) async-start(), calls=%async_computation.20 | async-start | bytes 81920 | tf_op jit(solution)/shard_map/reduce_scatter | solution.py:252
  423.6 333.2 %all-reduce.21.cloned.1.call-start = ((), (), s32[]{:S(2)}) async-start(), calls=%async_computation.25 | async-start | bytes 6422528 | tf_op jit(solution)/shard_map/psum | solution.py:271
  696.5 43.9 %copy-start.43 = (f32[1024]{0:T(1024)S(1)}, f32[1024]{0:T(1024)}, u32[]{:S(2)}) copy-start(f32[1024]{0:T(1024)} %get-tuple-element.641) | copy-start | bytes 12292
  696.5 59.4 %copy-start.49 = (f32[128]{0:T(128)S(1)}, f32[128]{0:T(128)}, u32[]{:S(2)}) copy-start(f32[128]{0:T(128)} %get-tuple-element.746) | copy-start | bytes 1540
  756.9 8.3 %copy-start.19 = (f32[256,704]{0,1:T(8,128)S(1)}, f32[256,704]{0,1:T(8,128)}, u32[]{:S(2)}) copy-start(f32[256,704]{0,1:T(8,128)} %get-tuple-element.1182) | copy-start | bytes 2162692
  756.9 9.2 %copy-start.18 = (f32[256,704]{0,1:T(8,128)S(1)}, f32[256,704]{0,1:T(8,128)}, u32[]{:S(2)}) copy-start(f32[256,704]{0,1:T(8,128)} %get-tuple-element.1183) | copy-start | bytes 2162692
  760.1 6.8 copy-start.17
  (28 other events, 66.6 us)
Sparse Core Ops, SparseCore 0:
  149.5 44.1 all-reduce.12
  260.2 43.5 all-reduce.16
  307.3 43.0 all-reduce.14
  414.5 43.8 all-reduce.18
  696.6 23.7 all-reduce.20
Sparse Core Ops, SparseCore 1:
  151.4 34.3 all-gather.7
  187.1 33.6 all-gather.9
  222.2 33.6 all-gather.11
  395.8 20.2 reduce-scatter.9
  419.0 20.1 reduce-scatter.11
  441.5 25.5 reduce-scatter.19
  469.2 25.7 reduce-scatter.13
  497.1 25.7 reduce-scatter.15
  525.1 54.8 reduce-scatter.21
  582.2 56.0 reduce-scatter.23
  640.4 56.0 reduce-scatter.25
  699.3 18.9 reduce-scatter.17
where the time goes:
time: 776 us; the launch traced here: 775 us
  waiting for transfers between devices  447 us (58%)
  blocking collectives  214 us (28%)
  matrix products  40.4 us (5%)
  other arithmetic  28.8 us (4%)
  local copies, waits for them, and re-layouts  25.7 us (3%)
  between operations  16.7 us (2%)
    reduce_scatter x1, waiting for transfers between devices, on_device(): lax.psum_scatter(d_up, 'seq', scatter_dimension=0, tiled=True)  58.4 us
    reduce_scatter x1, waiting for transfers between devices, on_device(): lax.psum_scatter(d_down, 'seq', scatter_dimension=1, tiled=True)  58.2 us
    reduce_scatter x1, waiting for transfers between devices, on_device(): lax.psum_scatter(d_gate, 'seq', scatter_dimension=0, tiled=True)  57 us
    psum x1, waiting for transfers between devices, on_device(): lax.psum(product(mlp_hidden, wdown_full).astype(jnp.bfloat16), 'head')  44.8 us
    psum x1, blocking collectives, on_device(): lax.psum((forget_full, bias_full, d_group), ('dp', 'seq', 'head'))  40.7 us
    psum x1, waiting for transfers between devices, on_device(): lax.psum(product(d_gate_pre, wgate_full.T) + product(d_up_pre, wup_full.T...  40.4 us
    all_gather x3, blocking collectives, entering(): gathered = jax.tree.map(lambda a: lax.all_gather(a, axis), part)  39 us
    dot_general x27, matrix products, product(): return jnp.dot(left, right, preferred_element_type=jnp.float32)  34.3 us
  transfers between devices with their start and end apart: 17, of which 12 were waited for; matrix products, arithmetic and copies ran while one was open for 4% of the time, Pallas kernels for 0%

commit v1 on v0

--- a/solution.py
+++ b/solution.py
@@ -290,7 +290,9 @@
     bias_full = lax.dynamic_update_slice_in_dim(
         jnp.zeros(forget_bias.shape, jnp.float32), d_bias, head_pos * key_cols, 0
     )
-    s_forget, s_bias, s_group = lax.psum((forget_full, bias_full, d_group), ("dp", "seq", "head"))
+    s_forget, s_bias, s_group = lax.psum(
+        lax.psum((forget_full, bias_full, d_group), axis_name="dp"), ("seq", "head")
+    )
     return (
         result.reshape(seqs_here, tok_here, width),
         grad_in.reshape(seqs_here, tok_here, width),

time: 776 us -> 818 us (1.054)
  blocking collectives: 214 us -> 248 us
  waiting for transfers between devices: 447 us -> 456 us
    psum x1, blocking collectives: 40.7 us -> 74.5 us  [on_device(): lax.psum(lax.psum((forget_full, bias_full, d_group), axis_name='dp'), ('s...]
  transfers between devices with their start and end apart: 17 -> 17, of which waited for: 12 -> 13; matrix products, arithmetic and copies ran while one was open for 4% -> 4% of each run, Pallas kernels for 0% -> 0%
where the time goes in v1:
time: 818 us; the launch traced here: 817 us
  waiting for transfers between devices  456 us (56%)
  blocking collectives  248 us (30%)
  matrix products  40.4 us (5%)
  other arithmetic  28.8 us (4%)
  local copies, waits for them, and re-layouts  25.7 us (3%)
  between operations  16.7 us (2%)
    psum x1, blocking collectives, on_device(): lax.psum(lax.psum((forget_full, bias_full, d_group), axis_name='dp'), ('s...  74.5 us
    reduce_scatter x1, waiting for transfers between devices, on_device(): lax.psum_scatter(d_up, 'seq', scatter_dimension=0, tiled=True)  58.4 us
    reduce_scatter x1, waiting for transfers between devices, on_device(): lax.psum_scatter(d_down, 'seq', scatter_dimension=1, tiled=True)  58.2 us
    reduce_scatter x1, waiting for transfers between devices, on_device(): lax.psum_scatter(d_gate, 'seq', scatter_dimension=0, tiled=True)  57 us
    psum x1, waiting for transfers between devices, on_device(): lax.psum(product(mlp_hidden, wdown_full).astype(jnp.bfloat16), 'head')  44.8 us
    psum x1, waiting for transfers between devices, on_device(): lax.psum(product(d_gate_pre, wgate_full.T) + product(d_up_pre, wup_full.T...  40.4 us
    all_gather x3, blocking collectives, entering(): gathered = jax.tree.map(lambda a: lax.all_gather(a, axis), part)  39 us
    dot_general x27, matrix products, product(): return jnp.dot(left, right, preferred_element_type=jnp.float32)  34.3 us
  transfers between devices with their start and end apart: 17, of which 13 were waited for; matrix products, arithmetic and copies ran while one was open for 4% of the time, Pallas kernels for 0%

profile of v1, /device:TPU:0, one launch (start us, length us, event | category | flops | bytes accessed | tf_op | source)
XLA Modules:
  0.0 816.5 jit_solution(14429585581531067307)
XLA Ops:
  10.6 12.6 %all-gather.2 = bf16[4,1,256]{2,1,0:T(2,128)(2,1)S(1)} all-gather(bf16[1,1,256]{2,1,0:T(2,128)(2,1)S(1)} %reshape.777), channel_id=1, replica_groups=mesh['dp'=2,'seq'=4,'head'=4] {'seq'}, dimensions={0}, use_global_device_ids=true | all-gather | bytes 2560 | tf_op jit(solution)/shard_map/all_gather | solution.py:115
  23.2 13.3 %all_gather.52 = bf16[1024,16]{0,1:T(8,128)(2,1)S(1)} all-gather(bf16[256,16]{0,1:T(8,128)(2,1)} %param.31), channel_id=1, replica_groups=mesh['dp'=2,'seq'=4,'head'=4] {'seq'}, dimensions={0}, use_global_device_ids=true | all-gather | bytes 40960 | tf_op jit(solution)/shard_map/all_gather | solution.py:120
  39.2 15.9 %all_gather.55 = bf16[1024,256]{1,0:T(8,128)(2,1)S(1)} all-gather(bf16[256,256]{1,0:T(8,128)(2,1)S(1)} %copy-done.37), channel_id=1, replica_groups=mesh['dp'=2,'seq'=4,'head'=4] {'seq'}, dimensions={0}, use_global_device_ids=true | all-gather | bytes 655360 | tf_op jit(solution)/shard_map/all_gather | solution.py:118
  55.4 14.5 %all_gather.54 = bf16[1024,128]{1,0:T(8,128)(2,1)S(1)} all-gather(bf16[256,128]{1,0:T(8,128)(2,1)S(1)} %copy-done.41), channel_id=1, replica_groups=mesh['dp'=2,'seq'=4,'head'=4] {'seq'}, dimensions={0}, use_global_device_ids=true | all-gather | bytes 327680 | tf_op jit(solution)/shard_map/all_gather | solution.py:117
  70.5 15.0 %all-gather = f32[512,256]{1,0:T(8,128)S(1)} all-gather(f32[128,256]{1,0:T(8,128)S(1)} %fusion.104), channel_id=2, replica_groups=mesh['dp'=2,'seq'=4,'head'=4] {'seq'}, dimensions={0}, use_global_device_ids=true | all-gather | bytes 655360 | tf_op jit(solution)/shard_map/all_gather | solution.py:18
  85.5 8.7 %all_gather.53 = f32[4,1,1,128]{3,2,1,0:T(1,128)S(1)} all-gather(f32[1,1,1,128]{3,2,1,0:T(1,128)S(1)} %get-tuple-element.748), channel_id=1, replica_groups=mesh['dp'=2,'seq'=4,'head'=4] {'seq'}, dimensions={0}, use_global_device_ids=true | all-gather | bytes 2560 | tf_op jit(solution)/shard_map/all_gather | solution.py:18
  94.2 14.6 %all_gather.58 = bf16[1024,128]{1,0:T(8,128)(2,1)S(1)} all-gather(bf16[256,128]{1,0:T(8,128)(2,1)S(1)} %copy-done.42), channel_id=1, replica_groups=mesh['dp'=2,'seq'=4,'head'=4] {'seq'}, dimensions={0}, use_global_device_ids=true | all-gather | bytes 327680 | tf_op jit(solution)/shard_map/all_gather | solution.py:116
  109.6 6.8 while.70
  110.3 1.7 fusion.282
  113.7 1.7 fusion.282
  117.1 15.5 %all_gather.59 = bf16[1024,256]{1,0:T(8,128)(2,1)S(1)} all-gather(bf16[256,256]{1,0:T(8,128)(2,1)S(1)} %copy-done.38), channel_id=1, replica_groups=mesh['dp'=2,'seq'=4,'head'=4] {'seq'}, dimensions={0}, use_global_device_ids=true | all-gather | bytes 655360 | tf_op jit(solution)/shard_map/all_gather | solution.py:119
  132.6 14.8 %all_gather.60 = bf16[256,1024]{1,0:T(8,128)(2,1)S(1)} all-gather(bf16[256,256]{1,0:T(8,128)(2,1)S(1)} %copy-done.39), channel_id=1, replica_groups=mesh['dp'=2,'seq'=4,'head'=4] {'seq'}, dimensions={1}, use_global_device_ids=true | all-gather | bytes 655360 | tf_op jit(solution)/shard_map/all_gather | solution.py:121
  151.2 8.8 %all-gather.3 = bf16[4,1,256]{2,1,0:T(2,128)(2,1)S(1)} all-gather(bf16[1,1,256]{2,1,0:T(2,128)(2,1)S(1)} %reshape.779), channel_id=1, replica_groups=mesh['dp'=2,'seq'=4,'head'=4] {'seq'}, dimensions={0}, use_global_device_ids=true | all-gather | bytes 2560 | tf_op jit(solution)/shard_map/all_gather | solution.py:122
  161.1 32.6 %all-reduce.13.cloned.1.call-done = f32[128,1024]{1,0:T(8,128)} async-done(((f32[128,1024]{1,0:T(8,128)}), f32[128,1024]{1,0:T(8,128)}) %all-reduce.13.cloned.1.call-update) | async-done | bytes 524304 | tf_op jit(solution)/shard_map/psum | solution.py:183
  195.6 2.7 fusion.132
  198.3 22.5 %all-gather.10.cloned.1.call-done = bf16[1024,704]{0,1:T(8,128)(2,1)} async-done(((bf16[256,704]{0,1:T(8,128)(2,1)}), bf16[1024,704]{0,1:T(8,128)(2,1)}) %all-gather.10.cloned.1.call-update) | async-done | bytes 1441808 | tf_op jit(solution)/shard_map/all_gather | solution.py:124
  220.8 2.6 fusion.133
  223.4 32.5 %all-gather.12.cloned.1.call-done = bf16[704,1024]{1,0:T(8,128)(2,1)} async-done(((bf16[704,256]{1,0:T(8,128)(2,1)}), bf16[704,1024]{1,0:T(8,128)(2,1)}) %all-gather.12.cloned.1.call-update) | async-done | bytes 1441808 | tf_op jit(solution)/shard_map/all_gather | solution.py:125
  255.9 2.2 multiply_convert_fusion.2
  260.9 2.5 convolution_convert_fusion
  263.4 40.4 %all-reduce.17.cloned.1.call-done = f32[128,1024]{1,0:T(8,128)} async-done(((f32[128,1024]{1,0:T(8,128)}), f32[128,1024]{1,0:T(8,128)}) %all-reduce.17.cloned.1.call-update) | async-done | bytes 524304 | tf_op jit(solution)/shard_map/psum | solution.py:203
  303.8 1.8 multiply_reduce_fusion.1
  305.6 44.8 %all-reduce.15.cloned.1.call-done = bf16[128,1024]{1,0:T(8,128)(2,1)} async-done(((bf16[128,1024]{1,0:T(8,128)(2,1)}), bf16[128,1024]{1,0:T(8,128)(2,1)}) %all-reduce.15.cloned.1.call-update) | async-done | bytes 262160 | tf_op jit(solution)/shard_map/psum | solution.py:191
  350.4 2.3 bitcast_add_fusion.7
  352.7 2.6 fusion.94
  355.7 15.3 %all-gather.1 = f32[512,256]{1,0:T(8,128)S(1)} all-gather(f32[128,256]{1,0:T(8,128)S(1)} %fusion.107), channel_id=3, replica_groups=mesh['dp'=2,'seq'=4,'head'=4] {'seq'}, dimensions={0}, use_global_device_ids=true | all-gather | bytes 655360 | tf_op jit(solution)/shard_map/all_gather | solution.py:18
  371.0 2.5 while.69
  374.3 19.5 %while.71 = (s32[]{:T(128)}, f32[1,1,128,256]{2,3,1,0:T(8,128)S(1)}, f32[2,1,1,64,128]{4,3,2,1,0:T(8,128)S(1)}, bf16[2,1,1,64,128]{4,3,2,1,0:T(8,128)(2,1)}, bf1...) while((s32[]{:T(128)}, ...), condition=%wide.region_23.24_spmd.clone.clone, body=%wide.region_16.23_spmd.clone.sunk.clone | while | flops 141848576 | bytes 4776213 | solution.py:76
  379.7 2.3 fusion.303
  389.4 2.3 fusion.303
  395.8 1.8 fusion.137
  402.0 2.1 fusion.140
  405.0 2.1 fusion.141
  408.2 2.1 fusion.124
  413.6 9.2 %psum.158 = bf16[128,16]{0,1:T(8,128)(2,1)S(1)} all-reduce(f32[128,16]{0,1:T(8,128)S(1)} %fusion.111), channel_id=1, replica_groups=mesh['dp'=2,'seq'=4,'head'=4] {'head'}, use_global_device_ids=true, to_apply=%region_25.26 | all-reduce | flops 2048 | bytes 12288 | tf_op jit(solution)/shard_map/psum | solution.py:239
  423.7 15.5 %reduce-scatter.12.cloned.1.call-done = f32[256,128]{1,0:T(8,128)} async-done(((f32[1024,128]{1,0:T(8,128)}), f32[256,128]{1,0:T(8,128)}) %reduce-scatter.12.cloned.1.call-update) | async-done | bytes 131088 | tf_op jit(solution)/shard_map/reduce_scatter | solution.py:249
  439.2 27.9 %reduce-scatter.20.cloned.1.call-done = f32[256,256]{1,0:T(8,128)} async-done(((f32[256,1024]{1,0:T(8,128)}), f32[256,256]{1,0:T(8,128)}) %reduce-scatter.20.cloned.1.call-update) | async-done | bytes 262160 | tf_op jit(solution)/shard_map/reduce_scatter | solution.py:253
  467.1 27.9 %reduce-scatter.14.cloned.1.call-done = f32[256,256]{1,0:T(8,128)} async-done(((f32[1024,256]{1,0:T(8,128)}), f32[256,256]{1,0:T(8,128)}) %reduce-scatter.14.cloned.1.call-update) | async-done | bytes 262160 | tf_op jit(solution)/shard_map/reduce_scatter | solution.py:250
  495.0 27.9 %reduce-scatter.16.cloned.1.call-done = f32[256,256]{1,0:T(8,128)} async-done(((f32[1024,256]{1,0:T(8,128)}), f32[256,256]{1,0:T(8,128)}) %reduce-scatter.16.cloned.1.call-update) | async-done | bytes 262160 | tf_op jit(solution)/shard_map/reduce_scatter | solution.py:251
  522.9 57.0 %reduce-scatter.22.cloned.1.call-done = f32[256,704]{0,1:T(8,128)} async-done(((f32[1024,704]{0,1:T(8,128)}), f32[256,704]{0,1:T(8,128)}) %reduce-scatter.22.cloned.1.call-update) | async-done | bytes 720912 | tf_op jit(solution)/shard_map/reduce_scatter | solution.py:255
  579.9 58.4 %reduce-scatter.24.cloned.1.call-done = f32[256,704]{0,1:T(8,128)} async-done(((f32[1024,704]{0,1:T(8,128)}), f32[256,704]{0,1:T(8,128)}) %reduce-scatter.24.cloned.1.call-update) | async-done | bytes 720912 | tf_op jit(solution)/shard_map/reduce_scatter | solution.py:256
  638.3 58.2 %reduce-scatter.26.cloned.1.call-done = f32[704,256]{1,0:T(8,128)} async-done(((f32[704,1024]{1,0:T(8,128)}), f32[704,256]{1,0:T(8,128)}) %reduce-scatter.26.cloned.1.call-update) | async-done | bytes 720912 | tf_op jit(solution)/shard_map/reduce_scatter | solution.py:257
  699.6 10.3 %all-reduce.4 = (f32[1024]{0:T(1024)S(1)}, f32[1024]{0:T(1024)S(1)}) all-reduce(f32[1024]{0:T(1024)S(1)} %get-tuple-element.643, f32[1024]{0:T(1024)S(1)} %copy-done.43), channel_id=4, replica_groups=mesh['dp'=2,'seq'=4,'head'=4] {'seq'}, use_global_device_ids=true, to_apply=%region_28.29.clone | all-reduce | flops 2048 | bytes 16384
  710.1 8.2 %reduce-scatter.18.cloned.1.call-done = f32[256,16]{0,1:T(8,128)} async-done(((f32[1024,16]{0,1:T(8,128)}), f32[256,16]{0,1:T(8,128)}) %reduce-scatter.18.cloned.1.call-update) | async-done | bytes 16400 | tf_op jit(solution)/shard_map/reduce_scatter | solution.py:252
  718.3 4.8 all-reduce.5
  723.0 74.5 %all-reduce.3 = (f32[16,512]{1,0:T(8,128)}, f32[512]{0:T(512)}, f32[256]{0:T(256)}) all-reduce(f32[16,512]{1,0:T(8,128)S(1)} %get-tuple-element.714, f32[512]{0:T(512)S(1)} %get-tuple-element.715, f32[256]{0:T(256)S(1)} %get-tuple-element.716), channel_id=1, replica_groups=mesh['dp'=2,'seq'=4,'head'=4] {'seq','head'}, use_global_device_ids=true, to_apply=%region_41.42 | all-reduce | flops 8960 | bytes 71680 | tf_op jit(solution)/shard_map/psum | solution.py:293
  798.5 1.7 copy.186
  801.8 1.7 copy.188
  (301 shorter events, 61.2 us)
Async XLA Ops:
  8.0 30.6 %copy-start = (f32[16,512]{1,0:T(8,128)S(1)}, f32[16,512]{1,0:T(8,128)}, u32[]{:S(2)}) copy-start(f32[16,512]{1,0:T(8,128)} %param.32) | copy-start | bytes 98308
  8.0 31.2 %copy-start.37 = (bf16[256,256]{1,0:T(8,128)(2,1)S(1)}, bf16[256,256]{1,0:T(8,128)(2,1)}, u32[]{:S(2)}) copy-start(bf16[256,256]{1,0:T(8,128)(2,1)} %param.29) | copy-start | bytes 393220
  8.0 47.3 %copy-start.41 = (bf16[256,128]{1,0:T(8,128)(2,1)S(1)}, bf16[256,128]{1,0:T(8,128)(2,1)}, u32[]{:S(2)}) copy-start(bf16[256,128]{1,0:T(8,128)(2,1)} %param.28) | copy-start | bytes 196612
  8.0 185.7 %all-reduce.13.cloned.1.call-start = ((), (), s32[]{:S(2)}) async-start(), calls=%async_computation.9 | async-start | bytes 1048576 | tf_op jit(solution)/shard_map/psum | solution.py:183
  9.9 250.8 %copy-start.44 = (f32[128]{0:T(128)}, f32[128]{0:T(128)S(1)}, u32[]{:S(2)}) copy-start(f32[128]{0:T(128)S(1)} %get-tuple-element.750) | copy-start | bytes 1540
  39.0 55.2 %copy-start.24 = (f32[128,128]{1,0:T(8,128)}, f32[128,128]{1,0:T(8,128)S(1)}, u32[]{:S(2)}) copy-start(f32[128,128]{1,0:T(8,128)S(1)} %convolution_add_fusion.7) | copy-start | bytes 196612
  55.4 38.8 %copy-start.42 = (bf16[256,128]{1,0:T(8,128)(2,1)S(1)}, bf16[256,128]{1,0:T(8,128)(2,1)}, u32[]{:S(2)}) copy-start(bf16[256,128]{1,0:T(8,128)(2,1)} %param.27) | copy-start | bytes 196612
  69.9 24.3 %copy-start.7 = (bf16[1024,128]{1,0:T(8,128)(2,1)}, bf16[1024,128]{1,0:T(8,128)(2,1)S(1)}, u32[]{:S(2)}) copy-start(bf16[1024,128]{1,0:T(8,128)(2,1)S(1)} %all_gather.54) | copy-start | bytes 786436
  94.2 15.3 %copy-start.46 = (f32[4,1,1,128]{3,2,1,0:T(1,128)}, f32[4,1,1,128]{3,2,1,0:T(1,128)S(1)}, u32[]{:S(2)}) copy-start(f32[4,1,1,128]{3,2,1,0:T(1,128)S(1)} %get-tuple-element.1290) | copy-start | bytes 6148
  109.1 8.0 copy-start.38
  109.1 23.5 %copy-start.39 = (bf16[256,256]{1,0:T(8,128)(2,1)S(1)}, bf16[256,256]{1,0:T(8,128)(2,1)}, u32[]{:S(2)}) copy-start(bf16[256,256]{1,0:T(8,128)(2,1)} %param.35) | copy-start | bytes 393220
  109.1 38.3 %copy-start.47 = (f32[256]{0:T(256)S(1)}, f32[256]{0:T(256)}, u32[]{:S(2)}) copy-start(f32[256]{0:T(256)} %param.34) | copy-start | bytes 3076
  116.4 33.0 %copy-start.29 = (f32[2,1,1,64,256]{4,3,2,1,0:T(8,128)}, f32[2,1,1,64,256]{4,3,2,1,0:T(8,128)S(1)}, u32[]{:S(2)}) copy-start(f32[2,1,1,64,256]{4,3,2,1,0:T(8,128)S(1)} %get-tuple-element.459) | copy-start | bytes 393220
  117.1 43.5 %copy-start.50 = (f32[128]{0:T(128)}, f32[128]{0:T(128)S(1)}, u32[]{:S(2)}) copy-start(f32[128]{0:T(128)S(1)} %rsqrt.38) | copy-start | bytes 1540
  132.6 17.9 %copy-start.9 = (bf16[1024,256]{1,0:T(8,128)(2,1)}, bf16[1024,256]{1,0:T(8,128)(2,1)S(1)}, u32[]{:S(2)}) copy-start(bf16[1024,256]{1,0:T(8,128)(2,1)S(1)} %all_gather.59) | copy-start | bytes 1572868
  147.4 47.5 %copy-start.11 = (bf16[256,1024]{1,0:T(8,128)(2,1)}, bf16[256,1024]{1,0:T(8,128)(2,1)S(1)}, u32[]{:S(2)}) copy-start(bf16[256,1024]{1,0:T(8,128)(2,1)S(1)} %all_gather.60) | copy-start | bytes 1572868
  147.4 46.3 %copy-start.1 = (f32[1,128,1024]{2,1,0:T(8,128)S(1)}, f32[1,128,1024]{2,1,0:T(8,128)}, u32[]{:S(2)}) copy-start(f32[1,128,1024]{2,1,0:T(8,128)} %param.24) | copy-start | bytes 1572868
  148.3 12.8 %copy-start.34 = (bf16[128,256]{1,0:T(8,128)(2,1)}, bf16[128,256]{1,0:T(8,128)(2,1)S(1)}, u32[]{:S(2)}) copy-start(bf16[128,256]{1,0:T(8,128)(2,1)S(1)} %get-tuple-element.753) | copy-start | bytes 196612
  149.4 46.2 %all-gather.8.cloned.1.call-start = ((), (), s32[]{:S(2)}) async-start(), calls=%async_computation.10 | async-start | bytes 1802240 | tf_op jit(solution)/shard_map/all_gather | solution.py:123
  149.9 70.9 %all-gather.10.cloned.1.call-start = ((), (), s32[]{:S(2)}) async-start(), calls=%async_computation.11 | async-start | bytes 1802240 | tf_op jit(solution)/shard_map/all_gather | solution.py:124
  150.5 105.4 %all-gather.12.cloned.1.call-start = ((), (), s32[]{:S(2)}) async-start(), calls=%async_computation.12 | async-start | bytes 1802240 | tf_op jit(solution)/shard_map/all_gather | solution.py:125
  151.1 152.7 %all-reduce.17.cloned.1.call-start = ((), (), s32[]{:S(2)}) async-start(), calls=%async_computation.14 | async-start | bytes 1048576 | tf_op jit(solution)/shard_map/psum | solution.py:203
  195.5 60.4 %copy-start.12 = (f32[1,128,1024]{2,1,0:T(8,128)S(1)}, f32[1,128,1024]{2,1,0:T(8,128)}, u32[]{:S(2)}) copy-start(f32[1,128,1024]{2,1,0:T(8,128)} %param.25) | copy-start | bytes 1572868
  260.1 90.3 %all-reduce.15.cloned.1.call-start = ((), (), s32[]{:S(2)}) async-start(), calls=%async_computation.13 | async-start | bytes 524288 | tf_op jit(solution)/shard_map/psum | solution.py:191
  263.3 89.4 %copy-start.30 = (f32[2,1,1,64,256]{4,3,2,1,0:T(8,128)S(1)}, f32[2,1,1,64,256]{4,3,2,1,0:T(8,128)}, u32[]{:S(2)}) copy-start(f32[2,1,1,64,256]{4,3,2,1,0:T(8,128)} %copy-done.29) | copy-start | bytes 393220
  263.3 89.4 %copy-start.51 = (f32[128]{0:T(128)S(1)}, f32[128]{0:T(128)}, u32[]{:S(2)}) copy-start(f32[128]{0:T(128)} %copy-done.50) | copy-start | bytes 1540
  263.4 160.3 %reduce-scatter.10.cloned.1.call-start = ((), (), s32[]{:S(2)}) async-start(), calls=%async_computation.16 | async-start | bytes 655360 | tf_op jit(solution)/shard_map/reduce_scatter | solution.py:248
  355.4 15.6 %copy-start.4 = (f32[128,256]{1,0:T(8,128)}, f32[128,256]{1,0:T(8,128)S(1)}, u32[]{:S(2)}) copy-start(f32[128,256]{1,0:T(8,128)S(1)} %fusion.91) | copy-start | bytes 393220
  374.3 5.0 copy-start.31
  376.6 6.6 copy-start.26
  386.3 6.6 copy-start.26
  395.8 43.4 %reduce-scatter.12.cloned.1.call-start = ((), (), s32[]{:S(2)}) async-start(), calls=%async_computation.17 | async-start | bytes 655360 | tf_op jit(solution)/shard_map/reduce_scatter | solution.py:249
  397.7 69.4 %reduce-scatter.20.cloned.1.call-start = ((), (), s32[]{:S(2)}) async-start(), calls=%async_computation.21 | async-start | bytes 1310720 | tf_op jit(solution)/shard_map/reduce_scatter | solution.py:253
  399.1 95.9 %reduce-scatter.14.cloned.1.call-start = ((), (), s32[]{:S(2)}) async-start(), calls=%async_computation.18 | async-start | bytes 1310720 | tf_op jit(solution)/shard_map/reduce_scatter | solution.py:250
  400.5 122.4 %reduce-scatter.16.cloned.1.call-start = ((), (), s32[]{:S(2)}) async-start(), calls=%async_computation.19 | async-start | bytes 1310720 | tf_op jit(solution)/shard_map/reduce_scatter | solution.py:251
  401.9 178.0 %reduce-scatter.22.cloned.1.call-start = ((), (), s32[]{:S(2)}) async-start(), calls=%async_computation.22 | async-start | bytes 3604480 | tf_op jit(solution)/shard_map/reduce_scatter | solution.py:255
  404.1 234.1 %reduce-scatter.24.cloned.1.call-start = ((), (), s32[]{:S(2)}) async-start(), calls=%async_computation.23 | async-start | bytes 3604480 | tf_op jit(solution)/shard_map/reduce_scatter | solution.py:256
  407.2 289.3 %reduce-scatter.26.cloned.1.call-start = ((), (), s32[]{:S(2)}) async-start(), calls=%async_computation.24 | async-start | bytes 3604480 | tf_op jit(solution)/shard_map/reduce_scatter | solution.py:257
  410.4 287.8 %all-reduce.19.cloned.1.call-start = ((), (), s32[]{:S(2)}) async-start(), calls=%async_computation.15 | async-start | bytes 1048576 | tf_op jit(solution)/shard_map/psum | solution.py:239
  413.3 283.2 %copy-start.54 = (u32[32]{0:T(128)S(1)}, u32[32]{0:T(128)}, u32[]{:S(2)}) copy-start(u32[32]{0:T(128)} %constant.207) | copy-start | bytes 388
  413.3 284.9 %copy-start.45 = (f32[128]{0:T(128)S(1)}, f32[128]{0:T(128)}, u32[]{:S(2)}) copy-start(f32[128]{0:T(128)} %copy-done.44) | copy-start | bytes 1540
  413.3 305.0 %reduce-scatter.18.cloned.1.call-start = ((), (), s32[]{:S(2)}) async-start(), calls=%async_computation.20 | async-start | bytes 81920 | tf_op jit(solution)/shard_map/reduce_scatter | solution.py:252
  423.6 374.9 %all-reduce.21.cloned.1.call-start = ((), (), s32[]{:S(2)}) async-start(), calls=%async_computation.25 | async-start | bytes 6422528 | tf_op jit(solution)/shard_map/psum | solution.py:271
  696.5 21.8 %copy-start.48 = (f32[256]{0:T(256)S(1)}, f32[256]{0:T(256)}, u32[]{:S(2)}) copy-start(f32[256]{0:T(256)} %get-tuple-element.645) | copy-start | bytes 3076
  696.5 101.1 %copy-start.49 = (f32[128]{0:T(128)S(1)}, f32[128]{0:T(128)}, u32[]{:S(2)}) copy-start(f32[128]{0:T(128)} %get-tuple-element.749) | copy-start | bytes 1540
  798.5 8.3 %copy-start.19 = (f32[256,704]{0,1:T(8,128)S(1)}, f32[256,704]{0,1:T(8,128)}, u32[]{:S(2)}) copy-start(f32[256,704]{0,1:T(8,128)} %get-tuple-element.1185) | copy-start | bytes 2162692
  798.5 9.2 %copy-start.18 = (f32[256,704]{0,1:T(8,128)S(1)}, f32[256,704]{0,1:T(8,128)}, u32[]{:S(2)}) copy-start(f32[256,704]{0,1:T(8,128)} %get-tuple-element.1186) | copy-start | bytes 2162692
  801.8 6.8 copy-start.17
  (28 other events, 64.7 us)
Sparse Core Ops, SparseCore 0:
  149.5 44.1 all-reduce.12
  260.2 43.5 all-reduce.16
  307.3 43.0 all-reduce.14
  414.5 43.8 all-reduce.18
  696.6 23.7 all-reduce.20
Sparse Core Ops, SparseCore 1:
  151.4 34.3 all-gather.7
  187.1 33.6 all-gather.9
  222.2 33.6 all-gather.11
  395.8 20.1 reduce-scatter.9
  418.9 20.2 reduce-scatter.11
  441.5 25.5 reduce-scatter.19
  469.2 25.7 reduce-scatter.13
  497.1 25.7 reduce-scatter.15
  525.1 54.8 reduce-scatter.21
  582.2 56.0 reduce-scatter.23
  640.4 56.0 reduce-scatter.25
  699.3 18.9 reduce-scatter.17
